TPU v7x, 512 devices: a whole 4x8x8 slice. The times are simulated.
512 devices in a mesh: prow: 32 (over y, x), pcol: 16 (over z, core).
Axes of the slice: x: 4, y: 8, z: 8, core: 2. Of those that a mesh axis runs over, the one named last changes fastest.
Arguments:
- matrix: bfloat16 [4, 8192, 4, 4096], P(None, 'prow', None, 'pcol'), may hold values from -6 to 6
- pivots: int32 [2, 256], replicated, may hold values from 0 to 32767, as said below
- lower_inverse: bfloat16 [2, 256, 256], replicated, as said below
- upper_inverse: bfloat16 [2, 256, 256], replicated, as said below
Outputs:
- factored: bfloat16 [4, 8192, 4, 4096], P(None, 'prow', None, 'pcol')
Inputs may be any that keep to these rules, and one draw needn't show every extreme that they name: For each panel k and each i, pivots[k, i] is either k * 256 + i or a row at or after (k + 1) * 256; entry 0 of each list is k * 256; the rows of one panel's list are distinct, and each list names row 32767. Each lower_inverse[k] is unit lower triangular. Each upper_inverse[k] is upper triangular with positive diagonal.
All inputs are finite; a program needn't handle non-finite values.
Results may differ from a plain program's by a relative error of at most 0.0079.
Values may be sent and summed in bfloat16 or wider, within the bound.
A program may use at most 64 MiB of HBM per device.

v0:
```python
import jax
import jax.numpy as jnp
from jax import lax
from jax.sharding import PartitionSpec as P


def spread(block, axis, source):
    block = jnp.where(lax.axis_index(axis) == source, block, jnp.zeros_like(block))
    return lax.psum(block, axis)


def local(matrix, pivots, lower_inverse, upper_inverse):
    row_count = lax.axis_size("prow")
    col_count = lax.axis_size("pcol")
    my_row = lax.axis_index("prow")
    my_col = lax.axis_index("pcol")
    blocks_down, block, blocks_across, _ = matrix.shape
    local_rows = blocks_down * block
    local_cols = blocks_across * block
    current = matrix.reshape(local_rows, local_cols)
    row_place = jnp.arange(local_rows)
    col_place = jnp.arange(local_cols)
    global_rows = (row_place // block * row_count + my_row) * block + row_place % block
    global_cols = (col_place // block * col_count + my_col) * block + col_place % block
    for panel in range(pivots.shape[0]):
        start = panel * block
        chosen = pivots[panel]
        block_row = chosen // block
        is_mine = block_row % row_count == my_row
        local_index = block_row // row_count * block + chosen % block
        safe_index = jnp.where(is_mine, local_index, 0)
        picked = jnp.where(is_mine[:, None], current[safe_index], jnp.zeros((), jnp.bfloat16))
        top_holder = panel % row_count
        top_first = panel // row_count * block
        is_top = my_row == top_holder
        top_local = current[top_first : top_first + block]
        incoming = lax.psum(picked, "prow").astype(jnp.float32)
        old_top = spread(top_local, "prow", top_holder)
        incoming = incoming.astype(jnp.bfloat16)
        target = jnp.where(is_mine, local_index, local_rows)
        current = current.at[target].set(old_top, mode="drop")
        top_now = current[top_first : top_first + block]
        current = current.at[top_first : top_first + block].set(
            jnp.where(is_top, incoming, top_now)
        )
        panel_holder = panel % col_count
        panel_first = panel // col_count * block
        panel_cols = current[:, panel_first : panel_first + block]
        factor = jnp.dot(
            panel_cols, upper_inverse[panel], preferred_element_type=jnp.float32
        ).astype(jnp.bfloat16)
        lower = spread(factor, "pcol", panel_holder)
        upper = jnp.dot(lower_inverse[panel], incoming, preferred_element_type=jnp.float32).astype(
            jnp.bfloat16
        )
        row_mask = global_rows >= start + block
        col_mask = global_cols >= start + block
        product = jnp.dot(lower, upper, preferred_element_type=jnp.float32)
        changed = (current.astype(jnp.float32) - product).astype(jnp.bfloat16)
        current = jnp.where(row_mask[:, None] & col_mask[None, :], changed, current)
        panel_now = current[:, panel_first : panel_first + block]
        is_panel = my_col == panel_holder
        current = current.at[:, panel_first : panel_first + block].set(
            jnp.where(is_panel & row_mask[:, None], lower, panel_now)
        )
        top_now = current[top_first : top_first + block]
        current = current.at[top_first : top_first + block].set(
            jnp.where(is_top & col_mask[None, :], upper, top_now)
        )
    return current.reshape(matrix.shape)


def solution(mesh):
    in_specs = (P(None, "prow", None, "pcol"), P(), P(), P())
    out_specs = P(None, "prow", None, "pcol")
    return jax.shard_map(local, mesh=mesh, in_specs=in_specs, out_specs=out_specs, check_vma=False)
```

profile of v0, /device:TPU:1, one launch (start us, length us, event | category | flops | bytes accessed | tf_op | source)
XLA Modules:
  0.0 609.7 jit_solution(5548198204034712789)
XLA Ops:
  6.5 0.8 and_select_fusion.5
  7.3 0.8 fusion.45
  8.1 2.1 copy.11
  10.2 1.3 slice_select_fusion.4
  11.5 0.9 copy.12
  12.4 1.2 gather_fusion
  13.5 0.9 broadcast_select_fusion.1
  14.5 0.0 all-reduce.7.cloned.1.call-start
  14.6 161.5 %all-reduce.13.cloned.1.call-done = (bf16[256,1024]{1,0:T(8,128)(2,1)}, bf16[256,1024]{1,0:T(8,128)(2,1)}) async-done(((bf16[256,1024]{1,0:T(8,128)(2,1)}, bf16[256,1024]{1,0:T(8,128)(2,1)}), (bf16[256,1024]{1,0:T(8,128)(2,1)}, bf16[256,1024]{1,0:T(8,128)(2,1)})) %all-reduce.13.cloned.1.call-update) | async-done | bytes 1048592 | tf_op jit(solution)/shard_map/psum | solution.py:9
  176.1 3.3 scatter_fusion
  179.5 0.2 fusion.8
  179.7 1.1 fusion
  180.8 0.0 all-reduce.11.cloned.1.call-start
  180.9 0.7 compare_reduce_fusion
  181.6 0.3 convolution_convert_fusion.1
  181.9 116.9 %all-reduce.7.cloned.1.call-done = bf16[1024,256]{1,0:T(8,128)(2,1)} async-done(((bf16[1024,256]{1,0:T(8,128)(2,1)}), bf16[1024,256]{1,0:T(8,128)(2,1)}) %all-reduce.7.cloned.1.call-update) | async-done | bytes 524304 | tf_op jit(solution)/shard_map/psum | solution.py:9
  298.9 3.4 and_select_fusion
  302.2 2.9 fusion.2
  305.2 2.3 broadcast_select_fusion.2
  307.5 3.4 gather_fusion.1
  310.9 0.9 broadcast_select_fusion
  311.8 0.0 all-reduce.9.cloned.1.call-start
  311.9 155.8 %all-reduce.11.cloned.1.call-done = (bf16[256,1024]{1,0:T(8,128)(2,1)}, bf16[256,1024]{1,0:T(8,128)(2,1)}) async-done(((bf16[256,1024]{1,0:T(8,128)(2,1)}, bf16[256,1024]{1,0:T(8,128)(2,1)}), (bf16[256,1024]{1,0:T(8,128)(2,1)}, bf16[256,1024]{1,0:T(8,128)(2,1)})) %all-reduce.11.cloned.1.call-update) | async-done | bytes 1048592 | tf_op jit(solution)/shard_map/psum | solution.py:9
  467.7 5.4 scatter_fusion.1
  473.1 2.0 fusion.6
  475.1 2.1 fusion.1
  477.3 0.3 convolution_convert_fusion
  477.6 117.9 %all-reduce.9.cloned.1.call-done = bf16[1024,256]{1,0:T(8,128)(2,1)} async-done(((bf16[1024,256]{1,0:T(8,128)(2,1)}), bf16[1024,256]{1,0:T(8,128)(2,1)}) %all-reduce.9.cloned.1.call-update) | async-done | bytes 524304 | tf_op jit(solution)/shard_map/psum | solution.py:9
  595.5 3.5 and_select_fusion.1
  599.1 1.1 fusion.3
  600.2 0.2 fusion.4
  600.4 2.8 reshape.658
  (32 shorter events, 0.3 us)
Async XLA Ops:
  6.5 169.6 %all-reduce.13.cloned.1.call-start = ((), (), s32[]{:S(2)}) async-start(), calls=%async_computation.3 | async-start | bytes 2097152 | tf_op jit(solution)/shard_map/psum | solution.py:9
  14.5 284.4 %all-reduce.7.cloned.1.call-start = ((), (), s32[]{:S(2)}) async-start(), calls=%async_computation | async-start | bytes 1048576 | tf_op jit(solution)/shard_map/psum | solution.py:9
  176.1 3.4 copy-start
  176.1 3.6 copy-start.5
  179.5 2.2 copy-start.4
  180.8 286.9 %all-reduce.11.cloned.1.call-start = ((), (), s32[]{:S(2)}) async-start(), calls=%async_computation.2 | async-start | bytes 2097152 | tf_op jit(solution)/shard_map/psum | solution.py:9
  298.9 3.4 copy-start.2
  311.8 283.7 %all-reduce.9.cloned.1.call-start = ((), (), s32[]{:S(2)}) async-start(), calls=%async_computation.1 | async-start | bytes 1048576 | tf_op jit(solution)/shard_map/psum | solution.py:9
  467.7 5.4 copy-start.1
  467.7 7.4 %copy-start.6 = (bf16[2,256,256]{2,1,0:T(8,128)(2,1)S(1)}, bf16[2,256,256]{2,1,0:T(8,128)(2,1)}, u32[]{:S(2)}) copy-start(bf16[2,256,256]{2,1,0:T(8,128)(2,1)} %param.19) | copy-start | bytes 786436
  595.5 3.5 copy-start.3
Sparse Core Ops, SparseCore 0:
  14.6 161.4 all-reduce.12
  181.0 117.8 all-reduce.6
  311.9 155.7 all-reduce.10
  477.4 118.0 all-reduce.8
where the time goes:
time: 610 us
  waiting for transfers between devices  552 us (90%)
  local copies, waits for them, and re-layouts  19.8 us (3%)
  other arithmetic  13.5 us (2%)
  between operations  13.3 us (2%)
  matrix products  10.8 us (2%)
    psum x4, waiting for transfers between devices, spread(): return lax.psum(block, axis)  552 us
  transfers between devices with their start and end apart: 4, of which 4 were waited for; matrix products, arithmetic and copies ran while one was open for 0% of the time, Pallas kernels for 0%

commit v1 on v0

--- a/solution.py
+++ b/solution.py
@@ -6,7 +6,7 @@
 
 def spread(block, axis, source):
     block = jnp.where(lax.axis_index(axis) == source, block, jnp.zeros_like(block))
-    return lax.psum(block, axis)
+    return jnp.sum(lax.all_gather(block, axis), axis=0)
 
 
 def local(matrix, pivots, lower_inverse, upper_inverse):

time: 610 us -> 797 us (1.31)
  waiting for transfers between devices: 552 us -> 687 us
  other arithmetic: 13.5 us -> 44.6 us
  local copies, waits for them, and re-layouts: 19.8 us -> 37.1 us
    all_gather x0 -> x4, waiting for transfers between devices: none -> 414 us  [spread(): return jnp.sum(lax.all_gather(block, axis), axis=0)]
    psum x4 -> x2, waiting for transfers between devices: 552 us -> 273 us  [local(): incoming = lax.psum(picked, 'prow').astype(jnp.float32)]
    reduce_sum x0 -> x4, other arithmetic: none -> 27.1 us  [spread(): return jnp.sum(lax.all_gather(block, axis), axis=0)]
    unnamed x16 -> x22, local copies, waits for them, and re-layouts: 3 us -> 12.4 us
  transfers between devices with their start and end apart: 4 -> 6, of which waited for: 4 -> 6; matrix products, arithmetic and copies ran while one was open for 0% -> 6% of each run, Pallas kernels for 0% -> 0%
where the time goes in v1:
time: 797 us
  waiting for transfers between devices  687 us (86%)
  other arithmetic  44.6 us (6%)
  local copies, waits for them, and re-layouts  37.1 us (5%)
  between operations  13.8 us (2%)
  matrix products  13.6 us (2%)
    all_gather x4, waiting for transfers between devices, spread(): return jnp.sum(lax.all_gather(block, axis), axis=0)  414 us
    psum x2, waiting for transfers between devices, local(): incoming = lax.psum(picked, 'prow').astype(jnp.float32)  273 us
    reduce_sum x4, other arithmetic, spread(): return jnp.sum(lax.all_gather(block, axis), axis=0)  27.1 us
  transfers between devices with their start and end apart: 6, of which 6 were waited for; matrix products, arithmetic and copies ran while one was open for 6% of the time, Pallas kernels for 0%

profile of v1, /device:TPU:1, one launch (start us, length us, event | category | flops | bytes accessed | tf_op | source)
XLA Modules:
  0.0 796.7 jit_solution(893697331869985858)
XLA Ops:
  6.5 1.3 slice_select_fusion.4
  9.0 2.1 copy.40
  11.2 1.2 gather_fusion
  13.5 147.8 %all-gather.8.cloned.1.call-done = bf16[32,256,1024]{2,1,0:T(8,128)(2,1)} async-done(((bf16[1,256,1024]{2,1,0:T(8,128)(2,1)}), bf16[32,256,1024]{2,1,0:T(8,128)(2,1)}) %all-gather.8.cloned.1.call-update) | async-done | bytes 16777232 | tf_op jit(solution)/shard_map/all_gather | solution.py:9
  161.3 9.1 %reduce_sum.48 = bf16[256,1024]{1,0:T(8,128)(2,1)S(1)} reduce(bf16[32,256,1024]{2,1,0:T(8,128)(2,1)} %all-gather.8.cloned.1.call-done, bf16[]{:T(256)} %constant.277.clone.1), dimensions={0}, to_apply=%region_0.1 | reduce | flops 8126464 | bytes 17301506 | tf_op jit(solution)/shard_map/reduce_sum | solution.py:9
  170.4 2.8 scatter_fusion
  173.3 2.6 copy.26
  175.8 140.6 %all-reduce.3.cloned.1.call-done = bf16[256,1024]{0,1:T(8,128)(2,1)} async-done(((bf16[256,1024]{0,1:T(8,128)(2,1)}), bf16[256,1024]{0,1:T(8,128)(2,1)}) %all-reduce.3.cloned.1.call-update) | async-done | bytes 524304 | tf_op jit(solution)/shard_map/psum | solution.py:37
  316.4 2.2 fusion.8
  318.6 2.2 fusion
  322.7 59.7 %all-gather.10.cloned.1.call-done = bf16[16384,256]{1,0:T(8,128)(2,1)} async-done(((bf16[1024,256]{1,0:T(8,128)(2,1)}), bf16[16384,256]{1,0:T(8,128)(2,1)}) %all-gather.10.cloned.1.call-update) | async-done | bytes 8388624 | tf_op jit(solution)/shard_map/all_gather | solution.py:9
  382.4 5.0 reduce_sum.49
  387.7 3.4 and_select_fusion
  391.1 2.6 fusion.2
  393.6 2.3 broadcast_select_fusion.1
  396.1 2.9 copy.29
  399.0 1.2 gather_fusion.1
  401.5 145.6 %all-gather.12.cloned.1.call-done = bf16[8192,1024]{0,1:T(8,128)(2,1)} async-done(((bf16[256,1024]{0,1:T(8,128)(2,1)}), bf16[8192,1024]{0,1:T(8,128)(2,1)}) %all-gather.12.cloned.1.call-update) | async-done | bytes 16777232 | tf_op jit(solution)/shard_map/all_gather | solution.py:9
  547.1 10.3 %copy.41 = bf16[128,8,32,256]{3,2,1,0:T(8,128)(2,1)S(1)} copy(bf16[128,8,32,256]{3,1,2,0:T(8,128)(2,1)} %bitcast.70) | data formatting | bytes 33554432
  557.4 8.1 %bitcast_reduce_fusion = bf16[256,1024]{0,1:T(8,128)(2,1)S(1)} fusion(bf16[128,8,32,256]{3,2,1,0:T(8,128)(2,1)S(1)} %copy.41), kind=kLoop, calls=%fused_computation.4 | loop fusion | flops 8126464 | bytes 17301504 | tf_op jit(solution)/shard_map/reduce_sum | solution.py:9
  565.7 2.8 scatter_fusion.1
  568.6 2.6 copy.34
  571.1 132.9 %all-reduce.5.cloned.1.call-done = bf16[256,1024]{0,1:T(8,128)(2,1)} async-done(((bf16[256,1024]{0,1:T(8,128)(2,1)}), bf16[256,1024]{0,1:T(8,128)(2,1)}) %all-reduce.5.cloned.1.call-update) | async-done | bytes 524304 | tf_op jit(solution)/shard_map/psum | solution.py:37
  704.0 2.0 fusion.6
  706.1 2.2 fusion.1
  709.6 60.5 %all-gather.14.cloned.1.call-done = bf16[16384,256]{1,0:T(8,128)(2,1)} async-done(((bf16[1024,256]{1,0:T(8,128)(2,1)}), bf16[16384,256]{1,0:T(8,128)(2,1)}) %all-gather.14.cloned.1.call-update) | async-done | bytes 8388624 | tf_op jit(solution)/shard_map/all_gather | solution.py:9
  770.1 5.0 reduce_sum.51
  775.3 3.4 and_select_fusion.1
  778.7 2.6 fusion.3
  781.3 2.0 fusion.4
  783.3 3.3 reshape.668
  786.6 3.2 copy.37
  (60 shorter events, 7.5 us)
Async XLA Ops:
  6.5 154.8 %all-gather.8.cloned.1.call-start = ((), (), s32[]{:S(2)}) async-start(), calls=%async_computation | async-start | bytes 17301504 | tf_op jit(solution)/shard_map/all_gather | solution.py:9
  9.0 307.4 %all-reduce.3.cloned.1.call-start = ((), (), s32[]{:S(2)}) async-start(), calls=%async_computation.1 | async-start | bytes 1048576 | tf_op jit(solution)/shard_map/psum | solution.py:37
  9.0 2.1 copy-start.7
  13.5 369.0 %all-gather.10.cloned.1.call-start = ((), (), s32[]{:S(2)}) async-start(), calls=%async_computation.3 | async-start | bytes 8912896 | tf_op jit(solution)/shard_map/all_gather | solution.py:9
  173.3 145.3 %copy-start.8 = (bf16[2,256,256]{2,1,0:T(8,128)(2,1)S(1)}, bf16[2,256,256]{2,1,0:T(8,128)(2,1)}, u32[]{:S(2)}) copy-start(bf16[2,256,256]{2,1,0:T(8,128)(2,1)} %param.19) | copy-start | bytes 786436
  175.8 145.7 %copy-start.6 = (bf16[2,256,256]{2,1,0:T(8,128)(2,1)S(1)}, bf16[2,256,256]{2,1,0:T(8,128)(2,1)}, u32[]{:S(2)}) copy-start(bf16[2,256,256]{2,1,0:T(8,128)(2,1)} %param.18) | copy-start | bytes 786436
  316.4 5.2 copy-start.2
  320.9 226.3 %all-gather.12.cloned.1.call-start = ((), (), s32[]{:S(2)}) async-start(), calls=%async_computation.4 | async-start | bytes 17301504 | tf_op jit(solution)/shard_map/all_gather | solution.py:9
  382.4 5.2 copy-start
  387.6 6.0 copy-start.4
  396.0 308.1 %all-reduce.5.cloned.1.call-start = ((), (), s32[]{:S(2)}) async-start(), calls=%async_computation.2 | async-start | bytes 1048576 | tf_op jit(solution)/shard_map/psum | solution.py:37
  401.2 368.8 %all-gather.14.cloned.1.call-start = ((), (), s32[]{:S(2)}) async-start(), calls=%async_computation.5 | async-start | bytes 8912896 | tf_op jit(solution)/shard_map/all_gather | solution.py:9
  568.6 137.5 %copy-start.9 = (bf16[2,256,256]{2,1,0:T(8,128)(2,1)S(1)}, bf16[2,256,256]{2,1,0:T(8,128)(2,1)}, u32[]{:S(2)}) copy-start(bf16[2,256,256]{2,1,0:T(8,128)(2,1)} %param.19) | copy-start | bytes 786436
  704.0 4.4 copy-start.3
  770.1 5.2 copy-start.1
  775.3 6.0 copy-start.5
Sparse Core Ops, SparseCore 0:
  10.5 150.7 all-gather.7
  164.7 151.6 all-reduce.2
  321.0 61.4 all-gather.9
  396.1 150.9 all-gather.11
  550.7 153.2 all-reduce.4
  708.4 61.5 all-gather.13
